TPU v7x, 256 devices: a whole 4x4x8 slice. The times are simulated.
256 devices in a mesh: grp: 4 (over y), col: 64 (over x, z, core).
Axes of the slice: x: 4, y: 4, z: 8, core: 2. Of those that a mesh axis runs over, the one named last changes fastest.
Arguments:
- inputs: bfloat16 [24, 256, 8192], P('grp', 'col'), may hold values from -6 to 6
- out_grads: bfloat16 [24, 256, 8192], P('grp', None, 'col'), may hold values from -0.5 to 0.5
- first_moment: float32 [8192, 8192], P(None, 'col'), may hold values from -2 to 2
- second_moment: float32 [8192, 8192], P(None, 'col'), may hold values from 0.01 to 1
- signs_in: int32 [8192], replicated, may hold values from 0 to 1
- signs_out: int32 [8192], replicated, may hold values from 0 to 1
- rows_in: int32 [64], replicated, may hold values from 0 to 8191, as said below
- rows_out: int32 [128], replicated, may hold values from 0 to 8191, as said below
- task_ids: int32 [24], P('grp'), may hold values from 0 to 7
- weights: int32 [24], P('grp'), may hold values from 1 to 4
Outputs:
- prototypes: float32 [8, 64, 128], P('grp', 'col')
Inputs may be any that keep to these rules, and one draw needn't show every extreme that they name: `rows_in`: distinct row numbers. `rows_out`: distinct row numbers.
All inputs are finite; a program needn't handle non-finite values.
Results may differ from a plain program's by a relative error of at most 0.0019.
Values may be sent and summed in bfloat16 or wider, within the bound.
A program may use at most 128 MiB of HBM per device.

v0:
```python
import math
import jax
import jax.numpy as jnp
from jax import lax
from jax.sharding import PartitionSpec as P

PRO_GRP = 2


def hadamard_rows(rows, sign_bits, cols, width):
    both = jnp.bitwise_and(rows[:, None], cols[None, :])
    parity = jnp.zeros(both.shape, jnp.int32)
    for bit in range(int(math.log2(width)) + 1):
        parity = jnp.bitwise_xor(parity, jnp.bitwise_and(jnp.right_shift(both, bit), 1))
    value = (1 - 2 * parity) * (1 - 2 * sign_bits)[None, :]
    return value.astype(jnp.float32)


def body(
    inputs,
    out_grads,
    first_moment,
    second_moment,
    signs_in,
    signs_out,
    rows_in,
    rows_out,
    task_ids,
    weights,
):
    width = first_moment.shape[0]
    n_col = lax.axis_size("col")
    n_grp = lax.axis_size("grp")
    grad = jnp.einsum(
        "etd,etc->edc",
        lax.all_gather(inputs, "col", axis=1, tiled=True),
        out_grads,
        preferred_element_type=jnp.float32,
    )
    first = 0.9 * first_moment[None] + 0.1 * grad
    second = 0.999 * second_moment[None] + 0.001 * grad * grad
    update = (first / (jnp.sqrt(second) + 1e-08)).astype(jnp.bfloat16)
    all_cols = jnp.arange(width, dtype=jnp.int32)
    left = hadamard_rows(rows_in, signs_in, all_cols, width).astype(jnp.bfloat16)
    half = jnp.einsum("rd,edc->erc", left, update, preferred_element_type=jnp.float32)
    right = hadamard_rows(rows_out, signs_out, all_cols, width)
    owned = lax.all_to_all(half, "col", split_axis=1, concat_axis=2, tiled=True)
    sketch = jnp.einsum("erd,kd->erk", owned, right, precision=lax.Precision.HIGHEST)
    entries = sketch.shape[1] * n_col * sketch.shape[2]
    squares = lax.psum(jnp.sum(sketch * sketch, axis=(1, 2)), "col")
    unit = sketch * lax.rsqrt(squares / entries + 1e-06)[:, None, None]
    n_proto = PRO_GRP * n_grp
    protos = jnp.arange(n_proto, dtype=jnp.int32)
    coef = jnp.where(
        task_ids[:, None] == protos[None, :], weights[:, None].astype(jnp.float32), jnp.float32(0.0)
    )
    term = jnp.einsum("ep,erk->prk", coef, unit, precision=lax.Precision.HIGHEST)
    return lax.psum_scatter(term, "grp", scatter_dimension=0, tiled=True)


def solution(mesh):
    placed = (
        P("grp", "col", None),
        P("grp", None, "col"),
        P(None, "col"),
        P(None, "col"),
        P(),
        P(),
        P(),
        P(),
        P("grp"),
        P("grp"),
    )
    return jax.shard_map(
        body, mesh=mesh, in_specs=placed, out_specs=P("grp", "col", None), check_vma=False
    )
```

profile of v0, /device:TPU:0, one launch (start us, length us, event | category | flops | bytes accessed | tf_op | source)
XLA Modules:
  0.0 381.7 jit_solution(12265177928836386276)
XLA Ops:
  6.5 0.0 copy-start
  6.5 0.0 all-gather.2.cloned.1.call-start
  6.5 2.1 copy.12
  8.6 0.0 all-gather.2.cloned.1.call-update
  8.6 0.8 multiply_subtract_fusion.1
  9.4 7.4 %broadcast_multiply_fusion = (f32[8192,128]{1,0:T(8,128)}, f32[8192,128]{1,0:T(8,128)}) fusion(f32[8192,128]{1,0:T(8,128)} %param.13, f32[8192,128]{1,0:T(8,128)} %param.12), kind=kLoop, calls=%fused_computation.74 | loop fusion | flops 2097152 | bytes 16777216 | tf_op jit(solution)/shard_map/mul | solution.py:41
  16.8 136.3 %all-gather.2.cloned.1.call-done = bf16[6,256,8192]{2,0,1:T(8,128)(2,1)} async-done(((bf16[6,4,8192]{2,0,1:T(8,128)(2,1)}), bf16[6,256,8192]{2,0,1:T(8,128)(2,1)}) %all-gather.2.cloned.1.call-update) | async-done | bytes 25165840 | tf_op jit(solution)/shard_map/all_gather | solution.py:36
  153.1 0.0 copy-done.2
  153.1 0.0 copy-start.1
  153.1 0.0 copy-start.4
  153.1 56.7 %fusion.76 = f32[6,64,128]{2,1,0:T(8,128)S(1)} fusion(bf16[6,256,128]{2,1,0:T(8,128)(2,1)S(1)} %copy-done, bf16[6,256,8192]{2,0,1:T(8,128)(2,1)} %all-gather.2.cloned.1.call-done, f32[8192,128]{1,0:T(8,128)} %get-tuple-element.7, f32[8192,128]{1,0:T(8,128)} %get-tuple-element.8, s32[8192]{0:T(1024)S(1)} %multiply_subtract_fusion.1, s32[64]{0:T(128)S(1)} %copy-done.2), kind=kOutput, calls=%fused_computation.76 | convolution fusion | flops 4101505024 | bytes 34177280 | tf_op jit(solution)/shard_map/rd,edc->erc/dot_general | solution.py:45
  209.9 0.8 copy.14
  210.7 6.2 %all-to-all-start = ((f32[6,64,128]{2,0,1:T(8,128)}), f32[6,64,128]{2,0,1:T(8,128)S(1)}, u32[]{:S(2)}, u32[]{:S(2)}) async-start(f32[6,64,128]{2,0,1:T(8,128)} %copy.14), calls=%async_computation | async-start | bytes 524288 | tf_op jit(solution)/shard_map/all_to_all | solution.py:47
  216.9 0.0 copy-done.3
  216.9 0.0 copy-done.6
  216.9 0.6 dynamic-slice
  218.1 0.0 copy-done.1
  218.2 0.0 copy-start.5
  218.2 10.7 %all-to-all-done = f32[6,64,128]{2,0,1:T(8,128)S(1)} async-done(((f32[6,64,128]{2,0,1:T(8,128)}), f32[6,64,128]{2,0,1:T(8,128)S(1)}, u32[]{:S(2)}, u32[]{:S(2)}) %all-to-all-start) | async-done | bytes 196640 | tf_op jit(solution)/shard_map/all_to_all | solution.py:47
  228.8 9.2 %multiply_reduce_fusion = (f32[6]{0:T(128)S(1)}, f32[6,128]{1,0:T(8,128)S(1)}) fusion(s32[8192]{0:T(1024)S(1)} %multiply_subtract_fusion, s32[128]{0:T(128)S(1)} %copy-done.4, f32[6,64,128]{2,0,1:T(8,128)S(1)} %all-to-all-done), kind=kOutput, calls=%fused_computation.99 | convolution fusion | flops 123733496 | bytes 232984 | tf_op jit(solution)/shard_map/erd,kd->erk/dot_general | solution.py:48
  238.0 125.5 %psum.7 = f32[6]{0:T(128)S(1)} all-reduce(f32[6]{0:T(128)S(1)} %get-tuple-element.5), channel_id=1, replica_groups=mesh['grp'=4,'col'=64] {'col'}, use_global_device_ids=true, to_apply=%region_1.0 | all-reduce | flops 6 | bytes 48 | tf_op jit(solution)/shard_map/psum | solution.py:50
  363.5 0.3 convolution_bitcast_fusion
  363.8 10.5 %all-reduce = f32[8,1,128]{2,0,1:T(8,128)S(1)} all-reduce(f32[8,1,128]{2,0,1:T(8,128)S(1)} %convolution_bitcast_fusion), channel_id=2, replica_groups=mesh['grp'=4,'col'=64] {'grp'}, use_global_device_ids=true, to_apply=%region_2.3.clone | all-reduce | flops 1024 | bytes 8192
  374.3 0.6 constant_dynamic-slice_fusion
  (9 shorter events, 0.0 us)
Async XLA Ops:
  6.5 146.6 %copy-start = (bf16[6,256,128]{2,1,0:T(8,128)(2,1)S(1)}, bf16[6,256,128]{2,1,0:T(8,128)(2,1)}, u32[]{:S(2)}) copy-start(bf16[6,256,128]{2,1,0:T(8,128)(2,1)} %param.11) | copy-start | bytes 1179652
  6.5 146.5 %all-gather.2.cloned.1.call-start = ((), (), s32[]{:S(2)}) async-start(), calls=%async_computation.1 | async-start | bytes 34078720 | tf_op jit(solution)/shard_map/all_gather | solution.py:36
  9.4 143.7 %copy-start.2 = (s32[64]{0:T(128)S(1)}, s32[64]{0:T(128)}, u32[]{:S(2)}) copy-start(s32[64]{0:T(128)} %param.16) | copy-start | bytes 772
  153.1 63.8 %copy-start.3 = (s32[6]{0:T(128)S(1)}, s32[6]{0:T(128)}, u32[]{:S(2)}) copy-start(s32[6]{0:T(128)} %param.19) | copy-start | bytes 76
  153.1 63.8 %copy-start.6 = (u32[256]{0:T(256)S(1)}, u32[256]{0:T(256)}, u32[]{:S(2)}) copy-start(u32[256]{0:T(256)} %constant.13) | copy-start | bytes 3076
  153.1 65.0 %copy-start.1 = (s32[8192]{0:T(1024)S(1)}, s32[8192]{0:T(1024)}, u32[]{:S(2)}) copy-start(s32[8192]{0:T(1024)} %param.15) | copy-start | bytes 98308
  153.1 75.7 %copy-start.4 = (s32[128]{0:T(128)S(1)}, s32[128]{0:T(128)}, u32[]{:S(2)}) copy-start(s32[128]{0:T(128)} %param.17) | copy-start | bytes 1540
  210.7 18.1 %all-to-all-start = ((f32[6,64,128]{2,0,1:T(8,128)}), f32[6,64,128]{2,0,1:T(8,128)S(1)}, u32[]{:S(2)}, u32[]{:S(2)}) async-start(f32[6,64,128]{2,0,1:T(8,128)} %copy.14), calls=%async_computation | async-start | bytes 524288 | tf_op jit(solution)/shard_map/all_to_all | solution.py:47
  218.2 145.4 %copy-start.5 = (s32[6]{0:T(128)S(1)}, s32[6]{0:T(128)}, u32[]{:S(2)}) copy-start(s32[6]{0:T(128)} %param.18) | copy-start | bytes 76
Sparse Core Ops, SparseCore 0:
  10.1 142.9 all-gather.1
where the time goes:
time: 382 us
  waiting for transfers between devices  147 us (38%)
  blocking collectives  136 us (36%)
  matrix products  66.2 us (17%)
  between operations  14.2 us (4%)
  other arithmetic  8.18 us (2%)
  starting transfers between devices  6.16 us (2%)
  local copies, waits for them, and re-layouts  4.09 us (1%)
    all_gather x1, waiting for transfers between devices, body(): lax.all_gather(inputs, 'col', axis=1, tiled=True)  136 us
    psum x1, blocking collectives, body(): squares = lax.psum(jnp.sum(sketch * sketch, axis=(1, 2)), 'col')  126 us
    dot_general x1, matrix products, body(): jnp.einsum('rd,edc->erc', left, update, preferred_element_type=jnp.float32)  56.7 us
    all_to_all x1, waiting for transfers between devices, body(): owned = lax.all_to_all(half, 'col', split_axis=1, concat_axis=2, tiled=True)  10.7 us
    unnamed x1, blocking collectives  10.5 us
    dot_general x1, matrix products, body(): jnp.einsum('erd,kd->erk', owned, right, precision=lax.Precision.HIGHEST)  9.18 us
  transfers between devices with their start and end apart: 2, of which 2 were waited for; matrix products, arithmetic and copies ran while one was open for 2% of the time, Pallas kernels for 0%

commit v1 on v0

--- a/solution.py
+++ b/solution.py
@@ -5,6 +5,11 @@
 from jax.sharding import PartitionSpec as P
 
 PRO_GRP = 2
+
+
+def gather_over(block, axis, d):
+    repeated = jnp.stack([block] * lax.axis_size(axis))
+    return jnp.concatenate(lax.all_to_all(repeated, axis, 0, 0), axis=d)
 
 
 def hadamard_rows(rows, sign_bits, cols, width):
@@ -32,10 +37,7 @@
     n_col = lax.axis_size("col")
     n_grp = lax.axis_size("grp")
     grad = jnp.einsum(
-        "etd,etc->edc",
-        lax.all_gather(inputs, "col", axis=1, tiled=True),
-        out_grads,
-        preferred_element_type=jnp.float32,
+        "etd,etc->edc", gather_over(inputs, "col", 1), out_grads, preferred_element_type=jnp.float32
     )
     first = 0.9 * first_moment[None] + 0.1 * grad
     second = 0.999 * second_moment[None] + 0.001 * grad * grad

time: 382 us -> 819 us (2.14)
  waiting for transfers between devices: 147 us -> 549 us
  local copies, waits for them, and re-layouts: 4.09 us -> 68.9 us
  matrix products: 66.2 us -> 35.5 us
  between operations: 14.2 us -> 0.8 us
  starting transfers between devices: 6.16 us -> 19.5 us
    all_to_all x0 -> x1, waiting for transfers between devices: none -> 539 us  [gather_over(): return jnp.concatenate(lax.all_to_all(repeated, axis, 0, 0), axis=d)]
    all_gather x1 -> x0, waiting for transfers between devices: 136 us -> none  [body(): lax.all_gather(inputs, 'col', axis=1, tiled=True)]
    reshape x0 -> x2, local copies, waits for them, and re-layouts: none -> 52.4 us  [gather_over(): return jnp.concatenate(lax.all_to_all(repeated, axis, 0, 0), axis=d)]
    dot_general x1, matrix products: 56.7 us -> 26 us  [body(): jnp.einsum('rd,edc->erc', left, update, preferred_element_type=jnp.float32)]
    another operation x0 -> x1, local copies, waits for them, and re-layouts: none -> 14.5 us  [gather_over(): repeated = jnp.stack([block] * lax.axis_size(axis))]
    all_to_all x0 -> x1, starting transfers between devices: none -> 10.6 us  [gather_over(): return jnp.concatenate(lax.all_to_all(repeated, axis, 0, 0), axis=d)]
  transfers between devices with their start and end apart: 2 -> 2, of which waited for: 2 -> 2; matrix products, arithmetic and copies ran while one was open for 2% -> 1% of each run, Pallas kernels for 0% -> 0%
where the time goes in v1:
time: 819 us; the launch traced here: 817 us
  waiting for transfers between devices  549 us (67%)
  blocking collectives  136 us (17%)
  local copies, waits for them, and re-layouts  68.9 us (8%)
  matrix products  35.5 us (4%)
  starting transfers between devices  19.5 us (2%)
    all_to_all x1, waiting for transfers between devices, gather_over(): return jnp.concatenate(lax.all_to_all(repeated, axis, 0, 0), axis=d)  539 us
    psum x1, blocking collectives, body(): squares = lax.psum(jnp.sum(sketch * sketch, axis=(1, 2)), 'col')  126 us
    reshape x2, local copies, waits for them, and re-layouts, gather_over(): return jnp.concatenate(lax.all_to_all(repeated, axis, 0, 0), axis=d)  52.4 us
    dot_general x1, matrix products, body(): jnp.einsum('rd,edc->erc', left, update, preferred_element_type=jnp.float32)  26 us
  transfers between devices with their start and end apart: 2, of which 2 were waited for; matrix products, arithmetic and copies ran while one was open for 1% of the time, Pallas kernels for 0%

profile of v1, /device:TPU:0, one launch (start us, length us, event | category | flops | bytes accessed | tf_op | source)
XLA Modules:
  0.0 817.5 jit_solution(8479183445325976991)
XLA Ops:
  0.0 0.0 copy-start
  0.0 14.5 %stack.2 = bf16[64,6,4,8192]{3,2,1,0:T(4,128)(2,1)} broadcast(bf16[6,4,8192]{2,1,0:T(4,128)(2,1)} %param.10), dimensions={1,2,3} | broadcast | bytes 25559040 | tf_op jit(solution)/shard_map/stack | solution.py:11
  14.5 10.6 %all-to-all-start = ((bf16[64,6,4,8192]{3,2,1,0:T(4,128)(2,1)}), bf16[64,6,4,8192]{3,2,1,0:T(4,128)(2,1)}, u32[]{:S(2)}, u32[]{:S(2)}) async-start(bf16[64,6,4,8192]{3,2,1,0:T(4,128)(2,1)} %stack.2), calls=%async_computation | async-start | bytes 50331648 | tf_op jit(solution)/shard_map/all_to_all | solution.py:12
  25.1 0.0 copy-done.2
  25.2 7.4 broadcast_multiply_fusion
  32.6 538.6 %all-to-all-done = bf16[64,6,4,8192]{3,2,1,0:T(4,128)(2,1)} async-done(((bf16[64,6,4,8192]{3,2,1,0:T(4,128)(2,1)}), bf16[64,6,4,8192]{3,2,1,0:T(4,128)(2,1)}, u32[]{:S(2)}, u32[]{:S(2)}) %all-to-all-start) | async-done | bytes 25165856 | tf_op jit(solution)/shard_map/all_to_all | solution.py:12
  571.2 17.6 %copy.15 = bf16[6,64,4,8192]{3,2,1,0:T(4,128)(2,1)} copy(bf16[6,64,4,8192]{3,2,0,1:T(4,128)(2,1)} %bitcast) | data formatting | bytes 50331648 | tf_op jit(solution)/shard_map/reshape | solution.py:12
  588.8 34.8 %reshape.37 = bf16[6,256,8192]{2,1,0:T(8,128)(2,1)} reshape(bf16[6,64,4,8192]{3,2,1,0:T(4,128)(2,1)} %copy.15) | data formatting | bytes 50331648 | tf_op jit(solution)/shard_map/reshape | solution.py:12
  623.6 0.0 copy-done
  623.6 0.0 copy-done.4
  623.6 0.0 copy-start.8
  623.6 0.0 copy-start.3
  623.6 0.0 copy-start.6
  623.6 26.0 %fusion.71 = f32[6,64,128]{2,1,0:T(8,128)S(1)} fusion(f32[8192,128]{1,0:T(8,128)} %get-tuple-element.7, f32[8192,128]{1,0:T(8,128)} %get-tuple-element.8, s32[8192]{0:T(1024)S(1)} %multiply_subtract_fusion.1, s32[64]{0:T(128)S(1)} %copy-done.4, bf16[6,256,8192]{2,1,0:T(8,128)(2,1)} %reshape.37, bf16[6,256,128]{2,1,0:T(8,128)(2,1)S(1)} %copy-done), kind=kOutput, calls=%fused_computation.74 | convolution fusion | flops 4101505024 | bytes 34177280 | tf_op jit(solution)/shard_map/rd,edc->erc/dot_general | solution.py:47
  649.6 0.8 copy.17
  650.5 8.9 %all-to-all-start.1 = ((f32[6,64,128]{2,0,1:T(8,128)}), f32[6,64,128]{2,0,1:T(8,128)S(1)}, u32[]{:S(2)}, u32[]{:S(2)}) async-start(f32[6,64,128]{2,0,1:T(8,128)} %copy.17), calls=%async_computation.1 | async-start | bytes 524288 | tf_op jit(solution)/shard_map/all_to_all | solution.py:49
  659.5 0.6 dynamic-slice
  660.7 0.0 copy-start.7
  660.7 10.5 %all-to-all-done.1 = f32[6,64,128]{2,0,1:T(8,128)S(1)} async-done(((f32[6,64,128]{2,0,1:T(8,128)}), f32[6,64,128]{2,0,1:T(8,128)S(1)}, u32[]{:S(2)}, u32[]{:S(2)}) %all-to-all-start.1) | async-done | bytes 196640 | tf_op jit(solution)/shard_map/all_to_all | solution.py:49
  671.2 9.2 %multiply_reduce_fusion = (f32[6]{0:T(128)S(1)}, f32[6,128]{1,0:T(8,128)S(1)}) fusion(s32[8192]{0:T(1024)S(1)} %multiply_subtract_fusion, s32[128]{0:T(128)S(1)} %copy-done.6, f32[6,64,128]{2,0,1:T(8,128)S(1)} %all-to-all-done.1), kind=kOutput, calls=%fused_computation.97 | convolution fusion | flops 123733496 | bytes 232984 | tf_op jit(solution)/shard_map/erd,kd->erk/dot_general | solution.py:50
  680.4 125.5 %psum.7 = f32[6]{0:T(128)S(1)} all-reduce(f32[6]{0:T(128)S(1)} %get-tuple-element.5), channel_id=1, replica_groups=mesh['grp'=4,'col'=64] {'col'}, use_global_device_ids=true, to_apply=%region_1.0 | all-reduce | flops 6 | bytes 48 | tf_op jit(solution)/shard_map/psum | solution.py:52
  805.9 0.3 convolution_bitcast_fusion
  806.2 10.7 %all-reduce = f32[8,1,128]{2,0,1:T(8,128)S(1)} all-reduce(f32[8,1,128]{2,0,1:T(8,128)S(1)} %convolution_bitcast_fusion), channel_id=2, replica_groups=mesh['grp'=4,'col'=64] {'grp'}, use_global_device_ids=true, to_apply=%region_2.3.clone | all-reduce | flops 1024 | bytes 8192
  816.9 0.6 constant_dynamic-slice_fusion
  (14 shorter events, 0.0 us)
Async XLA Ops:
  0.0 623.6 %copy-start = (bf16[6,256,128]{2,1,0:T(8,128)(2,1)S(1)}, bf16[6,256,128]{2,1,0:T(8,128)(2,1)}, u32[]{:S(2)}) copy-start(bf16[6,256,128]{2,1,0:T(8,128)(2,1)} %param.11) | copy-start | bytes 1179652
  14.5 10.6 %copy-start.2 = (s32[8192]{0:T(1024)S(1)}, s32[8192]{0:T(1024)}, u32[]{:S(2)}) copy-start(s32[8192]{0:T(1024)} %param.14) | copy-start | bytes 98308
  14.5 556.7 %all-to-all-start = ((bf16[64,6,4,8192]{3,2,1,0:T(4,128)(2,1)}), bf16[64,6,4,8192]{3,2,1,0:T(4,128)(2,1)}, u32[]{:S(2)}, u32[]{:S(2)}) async-start(bf16[64,6,4,8192]{3,2,1,0:T(4,128)(2,1)} %stack.2), calls=%async_computation | async-start | bytes 50331648 | tf_op jit(solution)/shard_map/all_to_all | solution.py:12
  588.8 34.8 %copy-start.4 = (s32[64]{0:T(128)S(1)}, s32[64]{0:T(128)}, u32[]{:S(2)}) copy-start(s32[64]{0:T(128)} %param.16) | copy-start | bytes 772
  623.6 35.8 %copy-start.5 = (s32[6]{0:T(128)S(1)}, s32[6]{0:T(128)}, u32[]{:S(2)}) copy-start(s32[6]{0:T(128)} %param.19) | copy-start | bytes 76
  623.6 35.9 %copy-start.8 = (u32[256]{0:T(256)S(1)}, u32[256]{0:T(256)}, u32[]{:S(2)}) copy-start(u32[256]{0:T(256)} %constant.13) | copy-start | bytes 3076
  623.6 37.1 %copy-start.3 = (s32[8192]{0:T(1024)S(1)}, s32[8192]{0:T(1024)}, u32[]{:S(2)}) copy-start(s32[8192]{0:T(1024)} %param.15) | copy-start | bytes 98308
  623.6 47.6 %copy-start.6 = (s32[128]{0:T(128)S(1)}, s32[128]{0:T(128)}, u32[]{:S(2)}) copy-start(s32[128]{0:T(128)} %param.17) | copy-start | bytes 1540
  650.5 20.7 %all-to-all-start.1 = ((f32[6,64,128]{2,0,1:T(8,128)}), f32[6,64,128]{2,0,1:T(8,128)S(1)}, u32[]{:S(2)}, u32[]{:S(2)}) async-start(f32[6,64,128]{2,0,1:T(8,128)} %copy.17), calls=%async_computation.1 | async-start | bytes 524288 | tf_op jit(solution)/shard_map/all_to_all | solution.py:49
  660.7 145.2 %copy-start.7 = (s32[6]{0:T(128)S(1)}, s32[6]{0:T(128)}, u32[]{:S(2)}) copy-start(s32[6]{0:T(128)} %param.18) | copy-start | bytes 76
  671.2 146.3 %copy-start.1 = (bf16[6,256,128]{2,1,0:T(8,128)(2,1)S(1)}, bf16[6,256,128]{2,1,0:T(8,128)(2,1)}, u32[]{:S(2)}) copy-start(bf16[6,256,128]{2,1,0:T(8,128)(2,1)} %param.11) | copy-start | bytes 1179652
